TPU v7x, 128 devices: a whole 4x4x4 slice. The times are simulated.
128 devices in a mesh: dom: 16 (over y, z), sub: 8 (over x, core).
Axes of the slice: x: 4, y: 4, z: 4, core: 2. Of those that a mesh axis runs over, the one named last changes fastest.
Arguments:
- features: bfloat16 [131072, 256], P(('dom', 'sub')), may hold values from -6 to 6
- cotangent: bfloat16 [131072, 256], P(('dom', 'sub')), may hold values from -6 to 6
- w_self_one: bfloat16 [256, 256], replicated, may hold values from -0.375 to 0.375
- w_nbr_one: bfloat16 [256, 256], replicated, may hold values from -0.375 to 0.375
- bias_one: float32 [256], replicated, may hold values from -4 to 4
- w_self_two: bfloat16 [256, 256], replicated, may hold values from -0.375 to 0.375
- w_nbr_two: bfloat16 [256, 256], replicated, may hold values from -0.375 to 0.375
- in_count: int32 [131072], P(('dom', 'sub')), may hold values from 0 to 7
- send_list: int32 [128, 128, 4], P(('dom', 'sub')), may hold values from 0 to 1023
- src_slot: int32 [128, 2048], P(('dom', 'sub')), may hold values from 0 to 1535
- dst_slot: int32 [128, 2048], P(('dom', 'sub')), may hold values from 0 to 1535
- edge_count: int32 [128], P(('dom', 'sub')), may hold values from 512 to 2048, as said below
Outputs:
- grad_features: bfloat16 [131072, 256], P(('dom', 'sub'))
- grad_weights: float32 [4, 256, 256], replicated
- grad_bias: float32 [256], replicated
Inputs may be any that keep to these rules, and one draw needn't show every extreme that they name: Each device's first edge_count slots are live; one device has all 2048 live in every draw.
All inputs are finite; a program needn't handle non-finite values.
Results may differ from a plain program's by a relative error of at most 0.0056.
Values may be sent and summed in bfloat16 or wider, within the bound.
A program may use at most 64 MiB of HBM per device.

v0:
```python
import math
import jax
import jax.numpy as jnp
from jax import lax
from jax.sharding import PartitionSpec as P


def to_mirrors(master_rows, send_list):
    picked_rows = jnp.take(master_rows, send_list[0], axis=0)
    feature_dim = master_rows.shape[1]
    received = lax.all_to_all(picked_rows, ("dom", "sub"), split_axis=0, concat_axis=0, tiled=True)
    return received.reshape(-1, feature_dim)


def to_masters(mirror_partial, send_list, node_dev):
    feature_dim = mirror_partial.shape[1]
    per_peer = send_list.shape[2]
    sectioned_rows = mirror_partial.reshape(-1, per_peer, feature_dim)
    received = lax.all_to_all(
        sectioned_rows, ("dom", "sub"), split_axis=0, concat_axis=0, tiled=True
    )
    flat_rows = received.reshape(-1, feature_dim)
    owners = send_list[0].reshape(-1)
    placing = (jnp.arange(node_dev, dtype=jnp.int32)[:, None] == owners[None, :]).astype(
        jnp.float32
    )
    return jnp.dot(
        placing, flat_rows, precision=lax.Precision.HIGHEST, preferred_element_type=jnp.float32
    )


def spread(slot_table, from_slot, into_slot, live_count):
    slot_total = slot_table.shape[0]
    edge_slots = from_slot.shape[0]
    feature_dim = slot_table.shape[1]
    block_rows = math.gcd(512, edge_slots)
    slot_ids = jnp.arange(slot_total, dtype=jnp.int32)[None, :]

    def one_block(turn_index, total):
        offset = turn_index * block_rows
        from_part = lax.dynamic_slice_in_dim(from_slot, offset, block_rows)
        into_part = lax.dynamic_slice_in_dim(into_slot, offset, block_rows)
        live_rows = (jnp.arange(block_rows, dtype=jnp.int32) + offset < live_count)[:, None]
        picking = ((from_part[:, None] == slot_ids) & live_rows).astype(slot_table.dtype)
        picked_rows = jnp.dot(picking, slot_table, preferred_element_type=jnp.float32).astype(
            slot_table.dtype
        )
        placing = (into_part[:, None] == slot_ids).astype(slot_table.dtype)
        return total + tdot(placing, picked_rows)

    start_total = jnp.zeros((slot_total, feature_dim), jnp.float32)
    block_count = edge_slots // block_rows
    return lax.fori_loop(0, block_count, one_block, start_total)


def tdot(left, right):
    return lax.dot_general(
        left, right, (((0,), (0,)), ((), ())), preferred_element_type=jnp.float32
    )


def dot_transposed(left, right):
    return lax.dot_general(
        left, right, (((1,), (1,)), ((), ())), preferred_element_type=jnp.float32
    )


def silu_grad(value):
    sigmoid_v = jax.nn.sigmoid(value)
    return sigmoid_v * (1.0 + value * (1.0 - sigmoid_v))


def shards(
    features,
    cotangent,
    w_self_one,
    w_nbr_one,
    bias_one,
    w_self_two,
    w_nbr_two,
    in_count,
    send_list,
    src_slot,
    dst_slot,
    edge_count,
):
    node_dev = features.shape[0]
    sources = src_slot[0]
    targets = dst_slot[0]
    live_count = edge_count[0]
    inverse = (1.0 / jnp.maximum(in_count, 1).astype(jnp.float32))[:, None]

    def gather_sum(master_rows, from_slot, into_slot):
        slot_table = jnp.concatenate([master_rows, to_mirrors(master_rows, send_list)], axis=0)
        partial_value = spread(slot_table, from_slot, into_slot, live_count)
        return partial_value[:node_dev] + to_masters(partial_value[node_dev:], send_list, node_dev)

    mean_one = (gather_sum(features, sources, targets) * inverse).astype(jnp.bfloat16)
    z_one = (
        jnp.dot(features, w_self_one, preferred_element_type=jnp.float32)
        + jnp.dot(mean_one, w_nbr_one, preferred_element_type=jnp.float32)
        + bias_one
    )
    h_one = jax.nn.silu(z_one).astype(jnp.bfloat16)
    message_two = (dot_transposed(cotangent, w_nbr_two) * inverse).astype(jnp.bfloat16)
    forward_sum = gather_sum(h_one, sources, targets)
    backward_sum = gather_sum(message_two, targets, sources)
    mean_two = (forward_sum * inverse).astype(jnp.bfloat16)
    late_self = tdot(h_one, cotangent)
    late_nbr = tdot(mean_two, cotangent)
    grad_h_one = dot_transposed(cotangent, w_self_two) + backward_sum
    grad_z_one = (grad_h_one * silu_grad(z_one)).astype(jnp.bfloat16)
    message_one = (dot_transposed(grad_z_one, w_nbr_one) * inverse).astype(jnp.bfloat16)
    early_self = tdot(features, grad_z_one)
    early_nbr = tdot(mean_one, grad_z_one)
    early_bias = jnp.sum(grad_z_one.astype(jnp.float32), axis=0)
    grad_features = (
        dot_transposed(grad_z_one, w_self_one) + gather_sum(message_one, targets, sources)
    ).astype(jnp.bfloat16)
    self_one, nbr_one, bias_sum, self_two, nbr_two = lax.psum(
        (early_self, early_nbr, early_bias, late_self, late_nbr), ("dom", "sub")
    )
    norm_factor = jnp.float32(node_dev * lax.axis_size("dom") * lax.axis_size("sub")) ** (-0.5)
    grad_weights = jnp.stack([self_one, nbr_one, self_two, nbr_two]) * norm_factor
    grad_bias = bias_sum * norm_factor
    return (grad_features, grad_weights, grad_bias)


def solution(mesh):
    return jax.shard_map(
        shards,
        mesh=mesh,
        in_specs=(
            P(("dom", "sub"), None),
            P(("dom", "sub"), None),
            P(),
            P(),
            P(),
            P(),
            P(),
            P(("dom", "sub")),
            P(("dom", "sub"), None, None),
            P(("dom", "sub"), None),
            P(("dom", "sub"), None),
            P(("dom", "sub")),
        ),
        out_specs=(P(("dom", "sub"), None), P(), P()),
        check_vma=False,
    )
```

profile of v0, /device:TPU:1, one launch (start us, length us, event | category | flops | bytes accessed | tf_op | source)
XLA Modules:
  0.0 453.2 jit_solution(3980596526978102994)
XLA Ops:
  16.2 11.9 %all-to-all-start = ((bf16[128,4,256]{2,1,0:T(4,128)(2,1)}), bf16[128,4,256]{2,1,0:T(4,128)(2,1)}, u32[]{:S(2)}, u32[]{:S(2)}) async-start(bf16[128,4,256]{2,1,0:T(4,128)(2,1)} %get-tuple-element.741), calls=%async_computation | async-start | bytes 524288 | tf_op jit(solution)/shard_map/all_to_all | solution.py:11
  29.0 9.7 %all-to-all-done = bf16[128,4,256]{2,1,0:T(4,128)(2,1)} async-done(((bf16[128,4,256]{2,1,0:T(4,128)(2,1)}), bf16[128,4,256]{2,1,0:T(4,128)(2,1)}, u32[]{:S(2)}, u32[]{:S(2)}) %all-to-all-start) | async-done | bytes 262176 | tf_op jit(solution)/shard_map/all_to_all | solution.py:11
  38.7 4.6 %all-to-all-start.2 = ((bf16[128,4,256]{2,1,0:T(4,128)(2,1)}), bf16[128,4,256]{2,1,0:T(4,128)(2,1)S(1)}, u32[]{:S(2)}, u32[]{:S(2)}) async-start(bf16[128,4,256]{2,1,0:T(4,128)(2,1)} %get-tuple-element.740), calls=%async_computation.2 | async-start | bytes 524288 | tf_op jit(solution)/shard_map/all_to_all | solution.py:11
  46.9 20.3 %while.60 = (s32[]{:T(128)}, f32[1536,256]{1,0:T(8,128)S(1)}, s32[2048]{0:T(1024)S(1)}, s32[2048]{0:T(1024)}, s32[]{:T(128)}, /*index=5*/bf16[1536,256]{1,0:T(8,...) while((s32[]{:T(128)}, f32[1536,256]{1,0:T(8,128)S(1)}, s32[2048]{0:T(1024)S(1)}, ...), condition=%wide.region_1.3_spmd.clone.clone, body=%wide.region_0.0_spmd.clone.clone.sunk | while | flops 808584192 | bytes 3945645 | solution.py:53
  48.4 3.6 fusion.125
  53.5 3.6 fusion.125
  58.6 3.6 fusion.125
  63.7 3.6 fusion.125
  68.7 9.8 %all-to-all-start.1 = ((f32[128,4,256]{2,1,0:T(4,128)}), f32[128,4,256]{2,1,0:T(4,128)S(1)}, u32[]{:S(2)}, u32[]{:S(2)}) async-start(f32[128,4,256]{2,1,0:T(4,128)} %reshape.79), calls=%async_computation.1 | async-start | bytes 1048576 | tf_op jit(solution)/shard_map/all_to_all | solution.py:19
  78.6 22.6 %while.61 = (s32[]{:T(128)}, f32[1536,256]{1,0:T(8,128)}, s32[2048]{0:T(1024)}, s32[2048]{0:T(1024)S(1)}, s32[]{:T(128)}, /*index=5*/bf16[1536,256]{1,0:T(8,128)...) while((s32[]{:T(128)}, f32[1536,256]{1,0:T(8,128)}, s32[2048]{0:T(1024)}, ...), condition=%wide.region_3.5_spmd.clone.clone, body=%wide.region_2.4_spmd.clone.clone.sunk | while | flops 808584192 | bytes 3945645 | solution.py:53
  84.7 4.5 fusion.128
  90.7 4.5 fusion.128
  96.7 4.5 fusion.128
  103.2 9.8 %all-to-all-start.3 = ((f32[128,4,256]{2,1,0:T(4,128)}), f32[128,4,256]{2,1,0:T(4,128)S(1)}, u32[]{:S(2)}, u32[]{:S(2)}) async-start(f32[128,4,256]{2,1,0:T(4,128)} %reshape.82), calls=%async_computation.3 | async-start | bytes 1048576 | tf_op jit(solution)/shard_map/all_to_all | solution.py:19
  117.8 8.8 %all-to-all-done.3 = f32[128,4,256]{2,1,0:T(4,128)S(1)} async-done(((f32[128,4,256]{2,1,0:T(4,128)}), f32[128,4,256]{2,1,0:T(4,128)S(1)}, u32[]{:S(2)}, u32[]{:S(2)}) %all-to-all-start.3) | async-done | bytes 524320 | tf_op jit(solution)/shard_map/all_to_all | solution.py:19
  139.1 4.6 %all-to-all-start.6 = ((bf16[128,4,256]{2,1,0:T(4,128)(2,1)}), bf16[128,4,256]{2,1,0:T(4,128)(2,1)S(1)}, u32[]{:S(2)}, u32[]{:S(2)}) async-start(bf16[128,4,256]{2,1,0:T(4,128)(2,1)} %get-tuple-element.738), calls=%async_computation.6 | async-start | bytes 524288 | tf_op jit(solution)/shard_map/all_to_all | solution.py:11
  144.8 67.1 %psum.39 = f32[256]{0:T(256)S(1)} all-reduce(f32[256]{0:T(256)S(1)} %copy-done.15), channel_id=1, replica_groups=mesh['dom'=16,'sub'=8] {'dom','sub'}, use_global_device_ids=true, to_apply=%region_13.15 | all-reduce | flops 256 | bytes 2048 | tf_op jit(solution)/shard_map/psum | solution.py:120
  212.5 4.7 %all-to-all-start.4 = ((bf16[128,4,256]{2,1,0:T(4,128)(2,1)}), bf16[128,4,256]{2,1,0:T(4,128)(2,1)S(1)}, u32[]{:S(2)}, u32[]{:S(2)}) async-start(bf16[128,4,256]{2,1,0:T(4,128)(2,1)} %get-tuple-element.739), calls=%async_computation.4 | async-start | bytes 524288 | tf_op jit(solution)/shard_map/all_to_all | solution.py:11
  218.2 21.7 %while.63 = (s32[]{:T(128)}, f32[1536,256]{1,0:T(8,128)}, s32[2048]{0:T(1024)S(1)}, s32[2048]{0:T(1024)S(1)}, s32[]{:T(128)}, /*index=5*/bf16[1536,256]{1,0:T(8,...) while((s32[]{:T(128)}, f32[1536,256]{1,0:T(8,128)}, s32[2048]{0:T(1024)S(1)}, ...), condition=%wide.region_10.12_spmd.clone.clone, body=%wide.region_9.11_spmd.clone.clone.sunk | while | flops 808584192 | bytes 3945645 | solution.py:53
  219.0 4.2 fusion.134
  224.0 4.7 %fusion.134 = f32[1536,256]{1,0:T(8,128)} fusion(f32[1536,256]{1,0:T(8,128)} %get-tuple-element.995, s32[512]{0:T(512)S(1)} %dynamic_slice.86, bf16[1536,256]{1,0:T(8,128)(2,1)} %get-tuple-element.1009, s32[512]{0:T(512)S(1)} %dynamic_slice.87, pred[512]{0:T(512)(128)(4,1)S(1)} %add_compare_fusion.11, pred[]{:T(512)S(6)} %compare.15), kind=kOutput, calls=%fused_computation.46.clone.1 | convolution fusion | flops 808583168 | bytes 3936769 | tf_op jit(solution)/shard_map/while/body/eval_jaxpr/dot_general | solution.py:57
  229.6 4.7 %fusion.134 = f32[1536,256]{1,0:T(8,128)} fusion(f32[1536,256]{1,0:T(8,128)} %get-tuple-element.995, s32[512]{0:T(512)S(1)} %dynamic_slice.86, bf16[1536,256]{1,0:T(8,128)(2,1)} %get-tuple-element.1009, s32[512]{0:T(512)S(1)} %dynamic_slice.87, pred[512]{0:T(512)(128)(4,1)S(1)} %add_compare_fusion.11, pred[]{:T(512)S(6)} %compare.15), kind=kOutput, calls=%fused_computation.46.clone.1 | convolution fusion | flops 808583168 | bytes 3936769 | tf_op jit(solution)/shard_map/while/body/eval_jaxpr/dot_general | solution.py:57
  235.1 4.7 %fusion.134 = f32[1536,256]{1,0:T(8,128)} fusion(f32[1536,256]{1,0:T(8,128)} %get-tuple-element.995, s32[512]{0:T(512)S(1)} %dynamic_slice.86, bf16[1536,256]{1,0:T(8,128)(2,1)} %get-tuple-element.1009, s32[512]{0:T(512)S(1)} %dynamic_slice.87, pred[512]{0:T(512)(128)(4,1)S(1)} %add_compare_fusion.11, pred[]{:T(512)S(6)} %compare.15), kind=kOutput, calls=%fused_computation.46.clone.1 | convolution fusion | flops 808583168 | bytes 3936769 | tf_op jit(solution)/shard_map/while/body/eval_jaxpr/dot_general | solution.py:57
  241.9 9.8 %all-to-all-start.7 = ((f32[128,4,256]{2,1,0:T(4,128)}), f32[128,4,256]{2,1,0:T(4,128)S(1)}, u32[]{:S(2)}, u32[]{:S(2)}) async-start(f32[128,4,256]{2,1,0:T(4,128)} %reshape.88), calls=%async_computation.7 | async-start | bytes 1048576 | tf_op jit(solution)/shard_map/all_to_all | solution.py:19
  252.7 21.8 %while.62 = (s32[]{:T(128)}, f32[1536,256]{1,0:T(8,128)}, s32[2048]{0:T(1024)S(1)}, s32[2048]{0:T(1024)S(1)}, s32[]{:T(128)}, /*index=5*/bf16[1536,256]{1,0:T(8,...) while((s32[]{:T(128)}, f32[1536,256]{1,0:T(8,128)}, s32[2048]{0:T(1024)S(1)}, ...), condition=%wide.region_5.7_spmd.clone.clone, body=%wide.region_4.6_spmd.clone.clone.sunk | while | flops 808584192 | bytes 3945645 | solution.py:53
  253.5 4.3 fusion.131
  258.6 4.8 %fusion.131 = f32[1536,256]{1,0:T(8,128)} fusion(f32[1536,256]{1,0:T(8,128)} %get-tuple-element.965, s32[512]{0:T(512)S(1)} %dynamic_slice.84, bf16[1536,256]{1,0:T(8,128)(2,1)} %get-tuple-element.979, s32[512]{0:T(512)S(1)} %dynamic_slice.85, pred[512]{0:T(512)(128)(4,1)S(1)} %add_compare_fusion.10, pred[]{:T(512)S(6)} %compare.14), kind=kOutput, calls=%fused_computation.35.clone.1 | convolution fusion | flops 808583168 | bytes 3936769 | tf_op jit(solution)/shard_map/while/body/eval_jaxpr/dot_general | solution.py:57
  264.1 4.8 %fusion.131 = f32[1536,256]{1,0:T(8,128)} fusion(f32[1536,256]{1,0:T(8,128)} %get-tuple-element.965, s32[512]{0:T(512)S(1)} %dynamic_slice.84, bf16[1536,256]{1,0:T(8,128)(2,1)} %get-tuple-element.979, s32[512]{0:T(512)S(1)} %dynamic_slice.85, pred[512]{0:T(512)(128)(4,1)S(1)} %add_compare_fusion.10, pred[]{:T(512)S(6)} %compare.14), kind=kOutput, calls=%fused_computation.35.clone.1 | convolution fusion | flops 808583168 | bytes 3936769 | tf_op jit(solution)/shard_map/while/body/eval_jaxpr/dot_general | solution.py:57
  269.7 4.8 %fusion.131 = f32[1536,256]{1,0:T(8,128)} fusion(f32[1536,256]{1,0:T(8,128)} %get-tuple-element.965, s32[512]{0:T(512)S(1)} %dynamic_slice.84, bf16[1536,256]{1,0:T(8,128)(2,1)} %get-tuple-element.979, s32[512]{0:T(512)S(1)} %dynamic_slice.85, pred[512]{0:T(512)(128)(4,1)S(1)} %add_compare_fusion.10, pred[]{:T(512)S(6)} %compare.14), kind=kOutput, calls=%fused_computation.35.clone.1 | convolution fusion | flops 808583168 | bytes 3936769 | tf_op jit(solution)/shard_map/while/body/eval_jaxpr/dot_general | solution.py:57
  276.5 9.8 %all-to-all-start.5 = ((f32[128,4,256]{2,1,0:T(4,128)}), f32[128,4,256]{2,1,0:T(4,128)S(1)}, u32[]{:S(2)}, u32[]{:S(2)}) async-start(f32[128,4,256]{2,1,0:T(4,128)} %reshape.85), calls=%async_computation.5 | async-start | bytes 1048576 | tf_op jit(solution)/shard_map/all_to_all | solution.py:19
  291.0 8.9 %all-to-all-done.5 = f32[128,4,256]{2,1,0:T(4,128)S(1)} async-done(((f32[128,4,256]{2,1,0:T(4,128)}), f32[128,4,256]{2,1,0:T(4,128)S(1)}, u32[]{:S(2)}, u32[]{:S(2)}) %all-to-all-start.5) | async-done | bytes 524320 | tf_op jit(solution)/shard_map/all_to_all | solution.py:19
  303.5 140.2 %all-reduce.3.cloned.1.call-done = (f32[1,256,256]{1,2,0:T(8,128)}, f32[1,256,256]{1,2,0:T(8,128)}, f32[1,256,256]{1,2,0:T(8,128)}, f32[1,256,256]{1,2,0:T(8,128)}) async-done(((f32[1,256,256]{1,2,0:T(8,128)}, f32[1,256,256]{1,2,0:T(8,128)}, f32[1,256,256]{1,2,0:T(8,128)}, f32[1,256,256]{1,2,0:T(8,128)}), (f32[1,256,256]{1,2,0:T(8,128)}, f32[1,256,256]{1,2,0:T(8,128)}, f32[1,256,256]{1,2,0:T(8,128)}, ...) | async-done | bytes 1048592 | tf_op jit(solution)/shard_map/psum | solution.py:120
  (150 shorter events, 74.0 us)
Async XLA Ops:
  7.2 2.4 copy-start
  10.8 2.0 copy-start.1
  14.8 13.4 %copy-start.12 = (s32[1,128,4]{1,2,0:T(4,128)S(1)}, s32[1,128,4]{1,2,0:T(4,128)}, u32[]{:S(2)}) copy-start(s32[1,128,4]{1,2,0:T(4,128)} %param.30) | copy-start | bytes 6148
  15.0 1.2 copy-start.10
  16.2 30.7 %copy-start.8 = (s32[1,2048]{1,0:T(1,128)S(1)}, s32[1,2048]{1,0:T(1,128)}, u32[]{:S(2)}) copy-start(s32[1,2048]{1,0:T(1,128)} %param.31) | copy-start | bytes 24580
  16.2 22.5 %all-to-all-start = ((bf16[128,4,256]{2,1,0:T(4,128)(2,1)}), bf16[128,4,256]{2,1,0:T(4,128)(2,1)}, u32[]{:S(2)}, u32[]{:S(2)}) async-start(bf16[128,4,256]{2,1,0:T(4,128)(2,1)} %get-tuple-element.741), calls=%async_computation | async-start | bytes 524288 | tf_op jit(solution)/shard_map/all_to_all | solution.py:11
  38.7 29.8 %all-to-all-start.2 = ((bf16[128,4,256]{2,1,0:T(4,128)(2,1)}), bf16[128,4,256]{2,1,0:T(4,128)(2,1)S(1)}, u32[]{:S(2)}, u32[]{:S(2)}) async-start(bf16[128,4,256]{2,1,0:T(4,128)(2,1)} %get-tuple-element.740), calls=%async_computation.2 | async-start | bytes 524288 | tf_op jit(solution)/shard_map/all_to_all | solution.py:11
  67.3 1.4 copy-start.2
  68.7 34.5 %all-to-all-start.1 = ((f32[128,4,256]{2,1,0:T(4,128)}), f32[128,4,256]{2,1,0:T(4,128)S(1)}, u32[]{:S(2)}, u32[]{:S(2)}) async-start(f32[128,4,256]{2,1,0:T(4,128)} %reshape.79), calls=%async_computation.1 | async-start | bytes 1048576 | tf_op jit(solution)/shard_map/all_to_all | solution.py:19
  101.2 11.8 %copy-start.7 = (bf16[256,256]{1,0:T(8,128)(2,1)S(1)}, bf16[256,256]{1,0:T(8,128)(2,1)}, u32[]{:S(2)}) copy-start(bf16[256,256]{1,0:T(8,128)(2,1)} %param.24) | copy-start | bytes 393220
  103.2 23.4 %all-to-all-start.3 = ((f32[128,4,256]{2,1,0:T(4,128)}), f32[128,4,256]{2,1,0:T(4,128)S(1)}, u32[]{:S(2)}, u32[]{:S(2)}) async-start(f32[128,4,256]{2,1,0:T(4,128)} %reshape.82), calls=%async_computation.3 | async-start | bytes 1048576 | tf_op jit(solution)/shard_map/all_to_all | solution.py:19
  113.0 1.5 copy-start.13
  117.8 11.3 %copy-start.4 = (f32[1024,256]{1,0:T(8,128)S(1)}, f32[1024,256]{1,0:T(8,128)}, u32[]{:S(2)}) copy-start(f32[1024,256]{1,0:T(8,128)} %fusion.82) | copy-start | bytes 3145732
  117.8 11.4 %copy-start.11 = (bf16[256,256]{1,0:T(8,128)(2,1)S(1)}, bf16[256,256]{1,0:T(8,128)(2,1)}, u32[]{:S(2)}) copy-start(bf16[256,256]{1,0:T(8,128)(2,1)} %param.25) | copy-start | bytes 393220
  129.2 1.3 copy-start.5
  129.2 1.4 copy-start.3
  129.2 1.4 copy-start.16
  137.1 6.6 %copy-start.6 = (bf16[1024,256]{1,0:T(8,128)(2,1)S(1)}, bf16[1024,256]{1,0:T(8,128)(2,1)}, u32[]{:S(2)}) copy-start(bf16[1024,256]{1,0:T(8,128)(2,1)} %copy-done.5) | copy-start | bytes 1572868
  137.2 7.6 %copy-start.15 = (f32[256]{0:T(256)S(1)}, f32[256]{0:T(256)}, u32[]{:S(2)}) copy-start(f32[256]{0:T(256)} %get-tuple-element.744) | copy-start | bytes 3076
  139.1 73.4 %all-to-all-start.6 = ((bf16[128,4,256]{2,1,0:T(4,128)(2,1)}), bf16[128,4,256]{2,1,0:T(4,128)(2,1)S(1)}, u32[]{:S(2)}, u32[]{:S(2)}) async-start(bf16[128,4,256]{2,1,0:T(4,128)(2,1)} %get-tuple-element.738), calls=%async_computation.6 | async-start | bytes 524288 | tf_op jit(solution)/shard_map/all_to_all | solution.py:11
  144.8 73.4 %copy-start.9 = (s32[2048]{0:T(1024)S(1)}, s32[2048]{0:T(1024)}, u32[]{:S(2)}) copy-start(s32[2048]{0:T(1024)} %get-tuple-element.1045) | copy-start | bytes 24580
  212.5 29.4 %all-to-all-start.4 = ((bf16[128,4,256]{2,1,0:T(4,128)(2,1)}), bf16[128,4,256]{2,1,0:T(4,128)(2,1)S(1)}, u32[]{:S(2)}, u32[]{:S(2)}) async-start(bf16[128,4,256]{2,1,0:T(4,128)(2,1)} %get-tuple-element.739), calls=%async_computation.4 | async-start | bytes 524288 | tf_op jit(solution)/shard_map/all_to_all | solution.py:11
  241.9 34.6 %all-to-all-start.7 = ((f32[128,4,256]{2,1,0:T(4,128)}), f32[128,4,256]{2,1,0:T(4,128)S(1)}, u32[]{:S(2)}, u32[]{:S(2)}) async-start(f32[128,4,256]{2,1,0:T(4,128)} %reshape.88), calls=%async_computation.7 | async-start | bytes 1048576 | tf_op jit(solution)/shard_map/all_to_all | solution.py:19
  276.5 11.1 %copy-start.14 = (s32[512]{0:T(512)S(1)}, s32[512]{0:T(512)}, u32[]{:S(2)}) copy-start(s32[512]{0:T(512)} %eq.293) | copy-start | bytes 6148
  276.5 23.4 %all-to-all-start.5 = ((f32[128,4,256]{2,1,0:T(4,128)}), f32[128,4,256]{2,1,0:T(4,128)S(1)}, u32[]{:S(2)}, u32[]{:S(2)}) async-start(f32[128,4,256]{2,1,0:T(4,128)} %reshape.85), calls=%async_computation.5 | async-start | bytes 1048576 | tf_op jit(solution)/shard_map/all_to_all | solution.py:19
  286.3 157.5 %all-reduce.3.cloned.1.call-start = ((), (), s32[]{:S(2)}) async-start(), calls=%async_computation.8 | async-start | bytes 2097152 | tf_op jit(solution)/shard_map/psum | solution.py:120
Sparse Core Ops, SparseCore 0:
  293.1 150.6 all-reduce.2
where the time goes:
time: 455 us; the launch traced here: 453 us
  waiting for transfers between devices  168 us (37%)
  matrix products  88.7 us (19%)
  blocking collectives  67.1 us (15%)
  starting transfers between devices  64.9 us (14%)
  local copies, waits for them, and re-layouts  28.8 us (6%)
  other arithmetic  21.3 us (5%)
  between operations  14.5 us (3%)
    psum x1, waiting for transfers between devices, shards(): lax.psum((early_self, early_nbr, early_bias, late_self, late_nbr), ('dom'...  140 us
    dot_general x20, matrix products, tdot(): lax.dot_general(left, right, (((0,), (0,)), ((), ())), preferred_element_...  72.1 us
    psum x1, blocking collectives, shards(): lax.psum((early_self, early_nbr, early_bias, late_self, late_nbr), ('dom'...  67.1 us
    all_to_all x4, starting transfers between devices, to_masters(): lax.all_to_all(sectioned_rows, ('dom', 'sub'), split_axis=0, concat_axis=...  39.1 us
    all_to_all x4, starting transfers between devices, to_mirrors(): lax.all_to_all(picked_rows, ('dom', 'sub'), split_axis=0, concat_axis=0,...  25.8 us
    all_to_all x4, waiting for transfers between devices, to_masters(): lax.all_to_all(sectioned_rows, ('dom', 'sub'), split_axis=0, concat_axis=...  17.7 us
    lt x16, other arithmetic, one_block(): jnp.arange(block_rows, dtype=jnp.int32) + offset < live_count  10.4 us
    dot_general x4, matrix products, to_masters(): jnp.dot(placing, flat_rows, precision=lax.Precision.HIGHEST, preferred_el...  10.2 us
  transfers between devices with their start and end apart: 9, of which 4 were waited for; matrix products, arithmetic and copies ran while one was open for 25% of the time, Pallas kernels for 0%

commit v1 on v0

--- a/solution.py
+++ b/solution.py
@@ -117,8 +117,12 @@
     grad_features = (
         dot_transposed(grad_z_one, w_self_one) + gather_sum(message_one, targets, sources)
     ).astype(jnp.bfloat16)
-    self_one, nbr_one, bias_sum, self_two, nbr_two = lax.psum(
-        (early_self, early_nbr, early_bias, late_self, late_nbr), ("dom", "sub")
+
+    def _connect_results(my_tile):
+        return lax.psum(lax.psum(my_tile, "sub"), "dom")
+
+    self_one, nbr_one, bias_sum, self_two, nbr_two = _connect_results(
+        (early_self, early_nbr, early_bias, late_self, late_nbr)
     )
     norm_factor = jnp.float32(node_dev * lax.axis_size("dom") * lax.axis_size("sub")) ** (-0.5)
     grad_weights = jnp.stack([self_one, nbr_one, self_two, nbr_two]) * norm_factor

time: 455 us -> 375 us (0.82)
  waiting for transfers between devices: 168 us -> 108 us
  blocking collectives: 67.1 us -> 47.8 us
  local copies, waits for them, and re-layouts: 28.8 us -> 34.5 us
  starting transfers between devices: 64.9 us -> 59.8 us
    psum x1 -> x2, waiting for transfers between devices: 140 us -> 70 us  [_connect_results(): return lax.psum(lax.psum(my_tile, 'sub'), 'dom')]
    psum x1 -> x2, blocking collectives: 67.1 us -> 47.8 us  [_connect_results(): return lax.psum(lax.psum(my_tile, 'sub'), 'dom')]
    all_to_all x4, waiting for transfers between devices: 9.69 us -> 18.6 us  [to_mirrors(): lax.all_to_all(picked_rows, ('dom', 'sub'), split_axis=0, concat_axis=0,...]
    all_to_all x4, starting transfers between devices: 39.1 us -> 33.9 us  [to_masters(): lax.all_to_all(sectioned_rows, ('dom', 'sub'), split_axis=0, concat_axis=...]
  transfers between devices with their start and end apart: 9 -> 10, of which waited for: 4 -> 6; matrix products, arithmetic and copies ran while one was open for 25% -> 31% of each run, Pallas kernels for 0% -> 0%
where the time goes in v1:
time: 375 us; the launch traced here: 372 us
  waiting for transfers between devices  108 us (29%)
  matrix products  85.7 us (23%)
  starting transfers between devices  59.8 us (16%)
  blocking collectives  47.8 us (13%)
  local copies, waits for them, and re-layouts  34.5 us (9%)
  other arithmetic  21.2 us (6%)
  between operations  14.5 us (4%)
    psum x2, waiting for transfers between devices, _connect_results(): return lax.psum(lax.psum(my_tile, 'sub'), 'dom')  70 us
    dot_general x20, matrix products, tdot(): lax.dot_general(left, right, (((0,), (0,)), ((), ())), preferred_element_...  68.9 us
    psum x2, blocking collectives, _connect_results(): return lax.psum(lax.psum(my_tile, 'sub'), 'dom')  47.8 us
    all_to_all x4, starting transfers between devices, to_masters(): lax.all_to_all(sectioned_rows, ('dom', 'sub'), split_axis=0, concat_axis=...  33.9 us
    all_to_all x4, starting transfers between devices, to_mirrors(): lax.all_to_all(picked_rows, ('dom', 'sub'), split_axis=0, concat_axis=0,...  25.6 us
    all_to_all x4, waiting for transfers between devices, to_masters(): lax.all_to_all(sectioned_rows, ('dom', 'sub'), split_axis=0, concat_axis=...  19.1 us
    all_to_all x4, waiting for transfers between devices, to_mirrors(): lax.all_to_all(picked_rows, ('dom', 'sub'), split_axis=0, concat_axis=0,...  18.6 us
    dot_general x4, matrix products, to_masters(): jnp.dot(placing, flat_rows, precision=lax.Precision.HIGHEST, preferred_el...  10.4 us
  transfers between devices with their start and end apart: 10, of which 6 were waited for; matrix products, arithmetic and copies ran while one was open for 31% of the time, Pallas kernels for 0%

profile of v1, /device:TPU:1, one launch (start us, length us, event | category | flops | bytes accessed | tf_op | source)
XLA Modules:
  0.0 371.6 jit_solution(474422452261983661)
XLA Ops:
  16.2 11.9 %all-to-all-start = ((bf16[128,4,256]{2,1,0:T(4,128)(2,1)}), bf16[128,4,256]{2,1,0:T(4,128)(2,1)}, u32[]{:S(2)}, u32[]{:S(2)}) async-start(bf16[128,4,256]{2,1,0:T(4,128)(2,1)} %get-tuple-element.745), calls=%async_computation | async-start | bytes 524288 | tf_op jit(solution)/shard_map/all_to_all | solution.py:11
  29.0 9.7 %all-to-all-done = bf16[128,4,256]{2,1,0:T(4,128)(2,1)} async-done(((bf16[128,4,256]{2,1,0:T(4,128)(2,1)}), bf16[128,4,256]{2,1,0:T(4,128)(2,1)}, u32[]{:S(2)}, u32[]{:S(2)}) %all-to-all-start) | async-done | bytes 262176 | tf_op jit(solution)/shard_map/all_to_all | solution.py:11
  38.7 4.6 %all-to-all-start.2 = ((bf16[128,4,256]{2,1,0:T(4,128)(2,1)}), bf16[128,4,256]{2,1,0:T(4,128)(2,1)S(1)}, u32[]{:S(2)}, u32[]{:S(2)}) async-start(bf16[128,4,256]{2,1,0:T(4,128)(2,1)} %get-tuple-element.744), calls=%async_computation.2 | async-start | bytes 524288 | tf_op jit(solution)/shard_map/all_to_all | solution.py:11
  46.9 20.3 %while.60 = (s32[]{:T(128)}, f32[1536,256]{1,0:T(8,128)S(1)}, s32[2048]{0:T(1024)S(1)}, s32[2048]{0:T(1024)}, s32[]{:T(128)}, /*index=5*/bf16[1536,256]{1,0:T(8,...) while((s32[]{:T(128)}, f32[1536,256]{1,0:T(8,128)S(1)}, s32[2048]{0:T(1024)S(1)}, ...), condition=%wide.region_1.3_spmd.clone.clone, body=%wide.region_0.0_spmd.clone.clone.sunk | while | flops 808584192 | bytes 3945645 | solution.py:53
  48.4 3.6 fusion.128
  53.5 3.6 fusion.128
  68.6 9.8 %all-to-all-start.1 = ((f32[128,4,256]{2,1,0:T(4,128)}), f32[128,4,256]{2,1,0:T(4,128)S(1)}, u32[]{:S(2)}, u32[]{:S(2)}) async-start(f32[128,4,256]{2,1,0:T(4,128)} %reshape.79), calls=%async_computation.1 | async-start | bytes 1048576 | tf_op jit(solution)/shard_map/all_to_all | solution.py:19
  78.5 22.7 %while.61 = (s32[]{:T(128)}, f32[1536,256]{1,0:T(8,128)}, s32[2048]{0:T(1024)}, s32[2048]{0:T(1024)S(1)}, s32[]{:T(128)}, /*index=5*/bf16[1536,256]{1,0:T(8,128)...) while((s32[]{:T(128)}, f32[1536,256]{1,0:T(8,128)}, s32[2048]{0:T(1024)}, ...), condition=%wide.region_3.5_spmd.clone.clone, body=%wide.region_2.4_spmd.clone.clone.sunk | while | flops 808584192 | bytes 3945645 | solution.py:53
  84.6 4.5 %fusion.131 = f32[1536,256]{1,0:T(8,128)} fusion(f32[1536,256]{1,0:T(8,128)} %get-tuple-element.909, s32[512]{0:T(512)S(1)} %dynamic_slice.82, bf16[1536,256]{1,0:T(8,128)(2,1)S(1)} %get-tuple-element.923, s32[512]{0:T(512)S(1)} %dynamic_slice.83, pred[512]{0:T(512)(128)(4,1)S(1)} %add_compare_fusion.9, pred[]{:T(512)S(6)} %compare.13), kind=kOutput, calls=%fused_computation.24.clone.1 | convolution fusion | flops 808583168 | bytes 3936769 | tf_op jit(solution)/shard_map/while/body/eval_jaxpr/dot_general | solution.py:57
  90.7 4.5 %fusion.131 = f32[1536,256]{1,0:T(8,128)} fusion(f32[1536,256]{1,0:T(8,128)} %get-tuple-element.909, s32[512]{0:T(512)S(1)} %dynamic_slice.82, bf16[1536,256]{1,0:T(8,128)(2,1)S(1)} %get-tuple-element.923, s32[512]{0:T(512)S(1)} %dynamic_slice.83, pred[512]{0:T(512)(128)(4,1)S(1)} %add_compare_fusion.9, pred[]{:T(512)S(6)} %compare.13), kind=kOutput, calls=%fused_computation.24.clone.1 | convolution fusion | flops 808583168 | bytes 3936769 | tf_op jit(solution)/shard_map/while/body/eval_jaxpr/dot_general | solution.py:57
  96.7 4.5 %fusion.131 = f32[1536,256]{1,0:T(8,128)} fusion(f32[1536,256]{1,0:T(8,128)} %get-tuple-element.909, s32[512]{0:T(512)S(1)} %dynamic_slice.82, bf16[1536,256]{1,0:T(8,128)(2,1)S(1)} %get-tuple-element.923, s32[512]{0:T(512)S(1)} %dynamic_slice.83, pred[512]{0:T(512)(128)(4,1)S(1)} %add_compare_fusion.9, pred[]{:T(512)S(6)} %compare.13), kind=kOutput, calls=%fused_computation.24.clone.1 | convolution fusion | flops 808583168 | bytes 3936769 | tf_op jit(solution)/shard_map/while/body/eval_jaxpr/dot_general | solution.py:57
  103.3 9.8 %all-to-all-start.3 = ((f32[128,4,256]{2,1,0:T(4,128)}), f32[128,4,256]{2,1,0:T(4,128)S(1)}, u32[]{:S(2)}, u32[]{:S(2)}) async-start(f32[128,4,256]{2,1,0:T(4,128)} %reshape.82), calls=%async_computation.3 | async-start | bytes 1048576 | tf_op jit(solution)/shard_map/all_to_all | solution.py:19
  117.8 8.8 %all-to-all-done.3 = f32[128,4,256]{2,1,0:T(4,128)S(1)} async-done(((f32[128,4,256]{2,1,0:T(4,128)}), f32[128,4,256]{2,1,0:T(4,128)S(1)}, u32[]{:S(2)}, u32[]{:S(2)}) %all-to-all-start.3) | async-done | bytes 524320 | tf_op jit(solution)/shard_map/all_to_all | solution.py:19
  138.9 4.6 %all-to-all-start.6 = ((bf16[128,4,256]{2,1,0:T(4,128)(2,1)}), bf16[128,4,256]{2,1,0:T(4,128)(2,1)S(1)}, u32[]{:S(2)}, u32[]{:S(2)}) async-start(bf16[128,4,256]{2,1,0:T(4,128)(2,1)} %get-tuple-element.742), calls=%async_computation.6 | async-start | bytes 524288 | tf_op jit(solution)/shard_map/all_to_all | solution.py:11
  145.7 8.9 %all-to-all-done.6 = bf16[128,4,256]{2,1,0:T(4,128)(2,1)S(1)} async-done(((bf16[128,4,256]{2,1,0:T(4,128)(2,1)}), bf16[128,4,256]{2,1,0:T(4,128)(2,1)S(1)}, u32[]{:S(2)}, u32[]{:S(2)}) %all-to-all-start.6) | async-done | bytes 262176 | tf_op jit(solution)/shard_map/all_to_all | solution.py:11
  154.6 4.5 %all-to-all-start.4 = ((bf16[128,4,256]{2,1,0:T(4,128)(2,1)}), bf16[128,4,256]{2,1,0:T(4,128)(2,1)S(1)}, u32[]{:S(2)}, u32[]{:S(2)}) async-start(bf16[128,4,256]{2,1,0:T(4,128)(2,1)} %get-tuple-element.743), calls=%async_computation.4 | async-start | bytes 524288 | tf_op jit(solution)/shard_map/all_to_all | solution.py:11
  160.1 24.4 %while.63 = (s32[]{:T(128)}, f32[1536,256]{1,0:T(8,128)}, s32[2048]{0:T(1024)}, s32[2048]{0:T(1024)S(1)}, s32[]{:T(128)}, /*index=5*/bf16[1536,256]{1,0:T(8,128)(2,1)}, s32[]{:T(128)}, s32[]{:T(128)}, s32[]{:T(128)}, s32[]{:T(128)}) while((s32[]{:T(128)}, f32[1536,256]{1,0:T(8,128)}, s32[2048]{0:T(1024)}, ...), condition=%wide.region_13.15_spmd.clone.clone, body=%wide.region_12.14_spmd.clone.clone.sunk | while | flops 808584192 | bytes 3945645 | solution.py:53
  161.6 4.2 %fusion.137 = f32[1536,256]{1,0:T(8,128)} fusion(f32[1536,256]{1,0:T(8,128)} %get-tuple-element.999, s32[512]{0:T(512)S(1)} %dynamic_slice.86, bf16[1536,256]{1,0:T(8,128)(2,1)} %get-tuple-element.1013, s32[512]{0:T(512)S(1)} %dynamic_slice.87, pred[512]{0:T(512)(128)(4,1)S(1)} %add_compare_fusion.11, pred[]{:T(512)S(6)} %compare.15), kind=kOutput, calls=%fused_computation.46.clone.1 | convolution fusion | flops 808583168 | bytes 3936769 | tf_op jit(solution)/shard_map/while/body/eval_jaxpr/dot_general | solution.py:57
  167.3 4.7 %fusion.137 = f32[1536,256]{1,0:T(8,128)} fusion(f32[1536,256]{1,0:T(8,128)} %get-tuple-element.999, s32[512]{0:T(512)S(1)} %dynamic_slice.86, bf16[1536,256]{1,0:T(8,128)(2,1)} %get-tuple-element.1013, s32[512]{0:T(512)S(1)} %dynamic_slice.87, pred[512]{0:T(512)(128)(4,1)S(1)} %add_compare_fusion.11, pred[]{:T(512)S(6)} %compare.15), kind=kOutput, calls=%fused_computation.46.clone.1 | convolution fusion | flops 808583168 | bytes 3936769 | tf_op jit(solution)/shard_map/while/body/eval_jaxpr/dot_general | solution.py:57
  173.5 4.7 %fusion.137 = f32[1536,256]{1,0:T(8,128)} fusion(f32[1536,256]{1,0:T(8,128)} %get-tuple-element.999, s32[512]{0:T(512)S(1)} %dynamic_slice.86, bf16[1536,256]{1,0:T(8,128)(2,1)} %get-tuple-element.1013, s32[512]{0:T(512)S(1)} %dynamic_slice.87, pred[512]{0:T(512)(128)(4,1)S(1)} %add_compare_fusion.11, pred[]{:T(512)S(6)} %compare.15), kind=kOutput, calls=%fused_computation.46.clone.1 | convolution fusion | flops 808583168 | bytes 3936769 | tf_op jit(solution)/shard_map/while/body/eval_jaxpr/dot_general | solution.py:57
  179.8 4.7 %fusion.137 = f32[1536,256]{1,0:T(8,128)} fusion(f32[1536,256]{1,0:T(8,128)} %get-tuple-element.999, s32[512]{0:T(512)S(1)} %dynamic_slice.86, bf16[1536,256]{1,0:T(8,128)(2,1)} %get-tuple-element.1013, s32[512]{0:T(512)S(1)} %dynamic_slice.87, pred[512]{0:T(512)(128)(4,1)S(1)} %add_compare_fusion.11, pred[]{:T(512)S(6)} %compare.15), kind=kOutput, calls=%fused_computation.46.clone.1 | convolution fusion | flops 808583168 | bytes 3936769 | tf_op jit(solution)/shard_map/while/body/eval_jaxpr/dot_general | solution.py:57
  186.5 9.8 %all-to-all-start.7 = ((f32[128,4,256]{2,1,0:T(4,128)}), f32[128,4,256]{2,1,0:T(4,128)S(1)}, u32[]{:S(2)}, u32[]{:S(2)}) async-start(f32[128,4,256]{2,1,0:T(4,128)} %reshape.88), calls=%async_computation.7 | async-start | bytes 1048576 | tf_op jit(solution)/shard_map/all_to_all | solution.py:19
  199.7 10.2 %all-to-all-done.7 = f32[128,4,256]{2,1,0:T(4,128)S(1)} async-done(((f32[128,4,256]{2,1,0:T(4,128)}), f32[128,4,256]{2,1,0:T(4,128)S(1)}, u32[]{:S(2)}, u32[]{:S(2)}) %all-to-all-start.7) | async-done | bytes 524320 | tf_op jit(solution)/shard_map/all_to_all | solution.py:19
  213.9 20.4 %while.62 = (s32[]{:T(128)}, f32[1536,256]{1,0:T(8,128)S(1)}, s32[2048]{0:T(1024)S(1)}, s32[2048]{0:T(1024)}, s32[]{:T(128)}, /*index=5*/bf16[1536,256]{1,0:T(8,...) while((s32[]{:T(128)}, f32[1536,256]{1,0:T(8,128)S(1)}, s32[2048]{0:T(1024)S(1)}, ...), condition=%wide.region_5.7_spmd.clone.clone, body=%wide.region_4.6_spmd.clone.clone.sunk | while | flops 808584192 | bytes 3945645 | solution.py:53
  215.4 3.6 fusion.134
  225.6 3.6 fusion.134
  230.7 3.6 fusion.134
  235.4 4.6 %all-to-all-start.5 = ((f32[128,4,256]{2,1,0:T(4,128)}), f32[128,4,256]{2,1,0:T(4,128)S(1)}, u32[]{:S(2)}, u32[]{:S(2)}) async-start(f32[128,4,256]{2,1,0:T(4,128)} %reshape.85), calls=%async_computation.5 | async-start | bytes 1048576 | tf_op jit(solution)/shard_map/all_to_all | solution.py:19
  240.1 30.7 %all-reduce.7.cloned.1.call-done = (f32[256,256]{0,1:T(8,128)}, f32[256,256]{0,1:T(8,128)}, f32[256,256]{0,1:T(8,128)}, f32[256,256]{0,1:T(8,128)}) async-done(((f32[256,256]{0,1:T(8,128)}, f32[256,256]{0,1:T(8,128)}, f32[256,256]{0,1:T(8,128)}, f32[256,256]{0,1:T(8,128)}), (f32[256,256]{0,1:T(8,128)}, f32[256,256]{0,1:T(8,128)}, f32[256,256]{0,1:T(8,128)}, ...) | async-done | bytes 1048592 | tf_op jit(solution)/shard_map/psum | solution.py:122
  270.8 14.3 %psum.78 = f32[256]{0:T(256)S(1)} all-reduce(f32[256]{0:T(256)S(1)} %copy-done.16), channel_id=1, replica_groups=mesh['dom'=16,'sub'=8] {'sub'}, use_global_device_ids=true, to_apply=%region_17.19 | all-reduce | flops 256 | bytes 2048 | tf_op jit(solution)/shard_map/psum | solution.py:122
  285.1 33.5 %psum.79 = f32[256]{0:T(256)S(1)} all-reduce(f32[256]{0:T(256)S(1)} %psum.78), channel_id=1, replica_groups=mesh['dom'=16,'sub'=8] {'dom'}, use_global_device_ids=true, to_apply=%region_18.20 | all-reduce | flops 256 | bytes 2048 | tf_op jit(solution)/shard_map/psum | solution.py:122
  322.9 39.3 %all-reduce.5.cloned.1.call-done = (f32[1,256,256]{1,2,0:T(8,128)}, f32[1,256,256]{1,2,0:T(8,128)}, f32[1,256,256]{1,2,0:T(8,128)}, f32[1,256,256]{1,2,0:T(8,128)}) async-done(((f32[1,256,256]{1,2,0:T(8,128)}, f32[1,256,256]{1,2,0:T(8,128)}, f32[1,256,256]{1,2,0:T(8,128)}, f32[1,256,256]{1,2,0:T(8,128)}), (f32[1,256,256]{1,2,0:T(8,128)}, f32[1,256,256]{1,2,0:T(8,128)}, f32[1,256,256]{1,2,0:T(8,128)}, ...) | async-done | bytes 1048592 | tf_op jit(solution)/shard_map/psum | solution.py:122
  (156 shorter events, 91.8 us)
Async XLA Ops:
  7.2 2.4 copy-start
  10.8 2.0 copy-start.1
  14.8 13.3 %copy-start.12 = (s32[1,128,4]{1,2,0:T(4,128)S(1)}, s32[1,128,4]{1,2,0:T(4,128)}, u32[]{:S(2)}) copy-start(s32[1,128,4]{1,2,0:T(4,128)} %param.30) | copy-start | bytes 6148
  15.0 1.2 copy-start.10
  16.2 30.7 %copy-start.9 = (s32[1,2048]{1,0:T(1,128)S(1)}, s32[1,2048]{1,0:T(1,128)}, u32[]{:S(2)}) copy-start(s32[1,2048]{1,0:T(1,128)} %param.31) | copy-start | bytes 24580
  16.2 22.5 %all-to-all-start = ((bf16[128,4,256]{2,1,0:T(4,128)(2,1)}), bf16[128,4,256]{2,1,0:T(4,128)(2,1)}, u32[]{:S(2)}, u32[]{:S(2)}) async-start(bf16[128,4,256]{2,1,0:T(4,128)(2,1)} %get-tuple-element.745), calls=%async_computation | async-start | bytes 524288 | tf_op jit(solution)/shard_map/all_to_all | solution.py:11
  38.7 29.8 %all-to-all-start.2 = ((bf16[128,4,256]{2,1,0:T(4,128)(2,1)}), bf16[128,4,256]{2,1,0:T(4,128)(2,1)S(1)}, u32[]{:S(2)}, u32[]{:S(2)}) async-start(bf16[128,4,256]{2,1,0:T(4,128)(2,1)} %get-tuple-element.744), calls=%async_computation.2 | async-start | bytes 524288 | tf_op jit(solution)/shard_map/all_to_all | solution.py:11
  67.2 1.4 copy-start.4
  68.6 34.7 %all-to-all-start.1 = ((f32[128,4,256]{2,1,0:T(4,128)}), f32[128,4,256]{2,1,0:T(4,128)S(1)}, u32[]{:S(2)}, u32[]{:S(2)}) async-start(f32[128,4,256]{2,1,0:T(4,128)} %reshape.79), calls=%async_computation.1 | async-start | bytes 1048576 | tf_op jit(solution)/shard_map/all_to_all | solution.py:19
  101.2 11.8 %copy-start.8 = (bf16[256,256]{1,0:T(8,128)(2,1)S(1)}, bf16[256,256]{1,0:T(8,128)(2,1)}, u32[]{:S(2)}) copy-start(bf16[256,256]{1,0:T(8,128)(2,1)} %param.24) | copy-start | bytes 393220
  103.3 23.4 %all-to-all-start.3 = ((f32[128,4,256]{2,1,0:T(4,128)}), f32[128,4,256]{2,1,0:T(4,128)S(1)}, u32[]{:S(2)}, u32[]{:S(2)}) async-start(f32[128,4,256]{2,1,0:T(4,128)} %reshape.82), calls=%async_computation.3 | async-start | bytes 1048576 | tf_op jit(solution)/shard_map/all_to_all | solution.py:19
  113.1 1.5 copy-start.13
  117.8 12.3 %copy-start.6 = (f32[1024,256]{1,0:T(8,128)S(1)}, f32[1024,256]{1,0:T(8,128)}, u32[]{:S(2)}) copy-start(f32[1024,256]{1,0:T(8,128)} %fusion.82) | copy-start | bytes 3145732
  117.8 12.3 %copy-start.11 = (bf16[256,256]{1,0:T(8,128)(2,1)S(1)}, bf16[256,256]{1,0:T(8,128)(2,1)}, u32[]{:S(2)}) copy-start(bf16[256,256]{1,0:T(8,128)(2,1)} %param.25) | copy-start | bytes 393220
  130.1 1.3 copy-start.7
  130.1 1.4 copy-start.5
  130.2 1.4 copy-start.17
  138.9 15.6 %all-to-all-start.6 = ((bf16[128,4,256]{2,1,0:T(4,128)(2,1)}), bf16[128,4,256]{2,1,0:T(4,128)(2,1)S(1)}, u32[]{:S(2)}, u32[]{:S(2)}) async-start(bf16[128,4,256]{2,1,0:T(4,128)(2,1)} %get-tuple-element.742), calls=%async_computation.6 | async-start | bytes 524288 | tf_op jit(solution)/shard_map/all_to_all | solution.py:11
  154.6 31.9 %all-to-all-start.4 = ((bf16[128,4,256]{2,1,0:T(4,128)(2,1)}), bf16[128,4,256]{2,1,0:T(4,128)(2,1)S(1)}, u32[]{:S(2)}, u32[]{:S(2)}) async-start(bf16[128,4,256]{2,1,0:T(4,128)(2,1)} %get-tuple-element.743), calls=%async_computation.4 | async-start | bytes 524288 | tf_op jit(solution)/shard_map/all_to_all | solution.py:11
  186.5 23.4 %all-to-all-start.7 = ((f32[128,4,256]{2,1,0:T(4,128)}), f32[128,4,256]{2,1,0:T(4,128)S(1)}, u32[]{:S(2)}, u32[]{:S(2)}) async-start(f32[128,4,256]{2,1,0:T(4,128)} %reshape.88), calls=%async_computation.7 | async-start | bytes 1048576 | tf_op jit(solution)/shard_map/all_to_all | solution.py:19
  196.3 74.5 %all-reduce.7.cloned.1.call-start = ((), (), s32[]{:S(2)}) async-start(), calls=%async_computation.9 | async-start | bytes 2097152 | tf_op jit(solution)/shard_map/psum | solution.py:122
  198.6 11.4 %copy-start.14 = (s32[512]{0:T(512)S(1)}, s32[512]{0:T(512)}, u32[]{:S(2)}) copy-start(s32[512]{0:T(512)} %eq.293) | copy-start | bytes 6148
  212.4 1.5 copy-start.2
  234.3 84.9 %copy-start.3 = (f32[1536,256]{1,0:T(8,128)}, f32[1536,256]{1,0:T(8,128)S(1)}, u32[]{:S(2)}) copy-start(f32[1536,256]{1,0:T(8,128)S(1)} %get-tuple-element.514) | copy-start | bytes 4718596
  234.3 36.5 %copy-start.16 = (f32[256]{0:T(256)S(1)}, f32[256]{0:T(256)}, u32[]{:S(2)}) copy-start(f32[256]{0:T(256)} %get-tuple-element.748) | copy-start | bytes 3076
  235.4 84.0 %copy-start.15 = (s32[512]{0:T(512)S(1)}, s32[512]{0:T(512)}, u32[]{:S(2)}) copy-start(s32[512]{0:T(512)} %eq.293) | copy-start | bytes 6148
  235.4 83.8 %all-to-all-start.5 = ((f32[128,4,256]{2,1,0:T(4,128)}), f32[128,4,256]{2,1,0:T(4,128)S(1)}, u32[]{:S(2)}, u32[]{:S(2)}) async-start(f32[128,4,256]{2,1,0:T(4,128)} %reshape.85), calls=%async_computation.5 | async-start | bytes 1048576 | tf_op jit(solution)/shard_map/all_to_all | solution.py:19
  240.0 122.1 %all-reduce.5.cloned.1.call-start = ((), (), s32[]{:S(2)}) async-start(), calls=%async_computation.8 | async-start | bytes 2097152 | tf_op jit(solution)/shard_map/psum | solution.py:122
Sparse Core Ops, SparseCore 0:
  213.6 57.0 all-reduce.6
  274.4 87.7 all-reduce.4
